TPU v7x, 32 devices: a whole 2x2x4 slice. The times are simulated.
32 devices in a mesh: group: 4 (over z), dp: 2 (over y), tensor: 4 (over x, core).
Axes of the slice: x: 2, y: 2, z: 4, core: 2. Of those that a mesh axis runs over, the one named last changes fastest.
Arguments:
- queries: bfloat16 [1024, 4096], P(('group', 'dp'), 'tensor'), may hold values from -16 to 16
- span_state: bfloat16 [1024, 4096], P(('group', 'dp'), 'tensor'), may hold values from -6 to 6
- neigh_state: bfloat16 [4096, 4096], P(('group', 'dp'), 'tensor'), may hold values from -24 to 24
- counts: int32 [4, 4], P('group'), may hold values from 1 to 2
- norm_gain: float32 [4096], P('tensor'), may hold values from 0.5 to 1.5
- head_gate: float32 [32], P('tensor'), may hold values from 0.3 to 1.5
- out_grad: bfloat16 [1024, 4096], P(('group', 'dp'), 'tensor'), may hold values from -6 to 6
Outputs:
- cross_output: bfloat16 [1024, 4096], P(('group', 'dp'), 'tensor')
- query_grad: bfloat16 [1024, 4096], P(('group', 'dp'), 'tensor')
- span_grad: bfloat16 [1024, 4096], P(('group', 'dp'), 'tensor')
- neighbour_grad: bfloat16 [4096, 4096], P(('group', 'dp'), 'tensor')
- gate_grad: float32 [32], P('tensor')
Inputs may be any that keep to these rules, and one draw needn't show every extreme that they name: Slot j of span c holds a retrieved neighbour exactly when j < counts[c].
All inputs are finite; a program needn't handle non-finite values.
Results may differ from a plain program's by a relative error of at most 0.0095.
The roundings to bfloat16 on the way count: a program that leaves them out, or rounds other values in their place, can miss the bound.
Values may be sent and summed in bfloat16 or wider, within the bound.
A program may use at most 64 MiB of HBM per device.

v0:
```python
import math

import jax
import jax.numpy as jnp
from jax import lax
from jax.sharding import PartitionSpec as P

CH = 64
NB = 2
NL = 128


epsilon = 1e-05
masked_score = -1e30


def shifted(value, axis, steps):
    count = lax.axis_size(axis)
    leading, last = (max(0, -steps), min(count, count - steps))
    return lax.ppermute(value, axis, [(source, source + steps) for source in range(leading, last)])


def product(form, left, right):
    return jnp.einsum(form, left, right, preferred_element_type=jnp.float32)


def encoder_forward(normed, neighbours, contexts):
    slot_count = normed.shape[1]
    spread = jnp.broadcast_to(
        contexts[:, None], (contexts.shape[0], slot_count) + contexts.shape[1:]
    )
    all_keys = jnp.concatenate([normed, spread], axis=2)
    scores = product("cjqhd,cjkhd->cjhqk", normed, all_keys) / normed.shape[-1]
    powers = jnp.exp(scores)
    weights = powers / jnp.sum(powers, axis=-1, keepdims=True)
    rounded = weights.astype(jnp.bfloat16)
    mixture = product("cjhqk,cjkhd->cjqhd", rounded, all_keys)
    encoded = (neighbours.astype(jnp.float32) + mixture).astype(jnp.bfloat16)
    return (encoded, (all_keys, weights, rounded, mixture))


def encoder_backward(grad_encoded, normed, saved):
    all_keys, weights, rounded, mixture = saved
    grad_rounded = grad_encoded.astype(jnp.bfloat16)
    grad_weights = product("cjqhd,cjkhd->cjhqk", grad_rounded, all_keys)
    offset = jnp.moveaxis(jnp.sum(grad_encoded * mixture, axis=-1), -1, 2)[..., None]
    score_grad = (weights * (grad_weights - offset) / normed.shape[-1]).astype(jnp.bfloat16)
    normed_grad = product("cjhqk,cjkhd->cjqhd", score_grad, all_keys)
    key_grad = product("cjhqk,cjqhd->cjkhd", score_grad, normed) + product(
        "cjhqk,cjqhd->cjkhd", rounded, grad_rounded
    )
    length = normed.shape[2]
    normed_grad = normed_grad + key_grad[:, :, :length]
    context_grad = jnp.sum(key_grad[:, :, length:], axis=1)
    return (normed_grad, context_grad)


def cross_attend(blocks, grad_blocks, keys, usable, present, gate_tanh):
    scale = 1.0 / math.sqrt(blocks.shape[-1])
    scores = product("brhd,bmhd->bhrm", blocks, keys) * scale
    scores = jnp.where(usable[:, None, None, :], scores, masked_score)
    highest = jnp.max(scores, axis=-1, keepdims=True)
    powers = jnp.exp(scores - highest)
    weights = powers / jnp.sum(powers, axis=-1, keepdims=True)
    rounded = weights.astype(jnp.bfloat16)
    attended = product("bhrm,bmhd->brhd", rounded, keys)
    present_mask = present[:, None, None, None]
    attended = jnp.where(present_mask, attended, 0.0)
    output = (gate_tanh[:, None] * attended).astype(jnp.bfloat16)
    grad_output = grad_blocks.astype(jnp.float32)
    gate_term = jnp.sum(grad_output * attended, axis=(0, 1, 3))
    att_grad = jnp.where(present_mask, gate_tanh[:, None] * grad_output, 0.0)
    grad_rounded = att_grad.astype(jnp.bfloat16)
    grad_weights = product("brhd,bmhd->bhrm", grad_rounded, keys)
    offset = jnp.moveaxis(jnp.sum(att_grad * attended, axis=-1), -1, 1)[..., None]
    score_grad = (weights * (grad_weights - offset) * scale).astype(jnp.bfloat16)
    query_grad = product("bhrm,bmhd->brhd", score_grad, keys).astype(jnp.bfloat16)
    key_grad = product("bhrm,brhd->bmhd", score_grad, blocks) + product(
        "bhrm,brhd->bmhd", rounded, grad_rounded
    )
    return (output, query_grad, key_grad, gate_term)


def shards(queries, span_state, neigh_state, counts, norm_gain, head_gate, out_grad):
    head_count = head_gate.shape[0]
    local_width = queries.shape[1]
    head_dim = local_width // head_count
    row_count = queries.shape[0]
    span_count = row_count // CH
    seq_spans = counts.shape[1]
    lead = CH - 1

    def blockify(matrix):
        return matrix.reshape(-1, CH, head_count, head_dim)

    neighbours = neigh_state.reshape(span_count, NB, NL, head_count, head_dim)
    contexts = span_state.reshape(span_count, CH, head_count, head_dim)
    gains = norm_gain.reshape(head_count, head_dim)
    floats = neighbours.astype(jnp.float32)
    square_sum = lax.psum(jnp.sum(floats * floats, axis=(3, 4)), "tensor")
    full_width = lax.axis_size("tensor") * local_width
    inverse = lax.rsqrt(square_sum / full_width + epsilon)[..., None, None]
    scaled = floats * inverse
    normed = (scaled * gains).astype(jnp.bfloat16)
    encoded, saved = encoder_forward(normed, neighbours, contexts)
    line_index = lax.axis_index("dp")
    first_span = line_index * span_count
    flat_counts = counts.reshape(-1)
    own_counts = lax.dynamic_slice_in_dim(flat_counts, first_span, span_count)
    gate_tanh = jnp.tanh(head_gate)
    usable = jnp.repeat(jnp.arange(NB)[None, :] < own_counts[:, None], NL, axis=1)
    present = own_counts > 0
    keys = encoded.reshape(span_count, NB * NL, head_count, head_dim)
    kept = row_count - lead
    incoming = shifted((queries[:lead], out_grad[:lead]), "dp", -1)
    follows = (first_span + span_count) % seq_spans != 0
    next_queries = jnp.where(follows, incoming[0], jnp.zeros_like(incoming[0]))
    next_grads = jnp.where(follows, incoming[1], jnp.zeros_like(incoming[1]))
    blocks = blockify(jnp.concatenate([queries[lead:], next_queries], axis=0))
    grad_blocks = blockify(jnp.concatenate([out_grad[lead:], next_grads], axis=0))
    local_out, local_query, key_grad, gate_terms = cross_attend(
        blocks, grad_blocks, keys, usable, present, gate_tanh
    )
    flat_out = local_out.reshape(row_count, local_width)
    flat_query = local_query.reshape(row_count, local_width)
    arrived = shifted((flat_out[kept:], flat_query[kept:]), "dp", 1)
    starts = first_span % seq_spans == 0
    front_out = jnp.where(starts, jnp.zeros_like(arrived[0]), arrived[0])
    front_query = jnp.where(starts, jnp.zeros_like(arrived[1]), arrived[1])
    cross_output = jnp.concatenate([front_out, flat_out[:kept]], axis=0)
    query_grad = jnp.concatenate([front_query, flat_query[:kept]], axis=0)
    grad_encoded = key_grad.reshape(span_count, NB, NL, head_count, head_dim)
    normed_grad, context_grad = encoder_backward(grad_encoded, normed, saved)
    gain_grad = normed_grad * gains
    projection = lax.psum(jnp.sum(gain_grad * scaled, axis=(3, 4)), "tensor") / full_width
    neighbour_grad = grad_encoded + inverse * (gain_grad - scaled * projection[..., None, None])
    total_tokens = lax.axis_size("group") * lax.axis_size("dp") * row_count
    summed = lax.psum(gate_terms, ("group", "dp"))
    gate_grad = (1.0 - gate_tanh * gate_tanh) * summed / math.sqrt(total_tokens)
    return (
        cross_output,
        query_grad,
        context_grad.reshape(row_count, local_width).astype(jnp.bfloat16),
        neighbour_grad.reshape(-1, local_width).astype(jnp.bfloat16),
        gate_grad,
    )


def solution(mesh):
    return jax.shard_map(
        shards,
        mesh=mesh,
        in_specs=(
            P(("group", "dp"), "tensor"),
            P(("group", "dp"), "tensor"),
            P(("group", "dp"), "tensor"),
            P("group", None),
            P("tensor"),
            P("tensor"),
            P(("group", "dp"), "tensor"),
        ),
        out_specs=(
            P(("group", "dp"), "tensor"),
            P(("group", "dp"), "tensor"),
            P(("group", "dp"), "tensor"),
            P(("group", "dp"), "tensor"),
            P("tensor"),
        ),
        check_vma=False,
    )
```

profile of v0, /device:TPU:0, one launch (start us, length us, event | category | flops | bytes accessed | tf_op | source)
XLA Modules:
  0.0 100.5 jit_solution(8903717577423482843)
XLA Ops:
  0.6 1.7 %slice.35 = bf16[63,1024]{1,0:T(8,128)(2,1)} slice(bf16[128,1024]{1,0:T(8,128)(2,1)} %param.13), slice={[0:63], [0:1024]} | slice | bytes 258048 | tf_op jit(solution)/shard_map/slice | solution.py:115
  2.3 1.3 %collective-permute-start.2 = (bf16[63,1024]{1,0:T(8,128)(2,1)}, bf16[63,1024]{1,0:T(8,128)(2,1)}, u32[]{:S(2)}, u32[]{:S(2)}) collective-permute-start(bf16[63,1024]{1,0:T(8,128)(2,1)} %slice.35), channel_id=1, source_target_pairs={{4,0},{5,1},{6,2},{7,3},{12,8},{13,9},{14,10},{15,11},{20,16},{21,... | collective-permute-start | bytes 387080 | tf_op jit(solution)/shard_map/ppermute | solution.py:20
  3.6 1.6 %slice.31 = bf16[63,1024]{1,0:T(8,128)(2,1)} slice(bf16[128,1024]{1,0:T(8,128)(2,1)} %param.7), slice={[0:63], [0:1024]} | slice | bytes 258048 | tf_op jit(solution)/shard_map/slice | solution.py:115
  5.2 1.3 %collective-permute-start = (bf16[63,1024]{1,0:T(8,128)(2,1)}, bf16[63,1024]{1,0:T(8,128)(2,1)}, u32[]{:S(2)}, u32[]{:S(2)}) collective-permute-start(bf16[63,1024]{1,0:T(8,128)(2,1)} %slice.31), channel_id=1, source_target_pairs={{4,0},{5,1},{6,2},{7,3},{12,8},{13,9},{14,10},{15,11},{20,16},{21,... | collective-permute-start | bytes 387080 | tf_op jit(solution)/shard_map/ppermute | solution.py:20
  6.5 0.9 slice.30
  7.4 0.9 slice.34
  8.4 1.5 %fusion.3 = f32[512]{0:T(512)S(1)} fusion(bf16[512,1024]{1,0:T(8,128)(2,1)} %param.9), kind=kLoop, calls=%fused_computation.8 | loop fusion | flops 1572352 | bytes 1050624 | tf_op jit(solution)/shard_map/reduce_sum | solution.py:100
  10.0 1.6 %convert_bitcast_fusion = f32[64,8,8,128]{3,1,2,0:T(8,128)} fusion(bf16[512,1024]{1,0:T(8,128)(2,1)S(1)} %copy-done.3), kind=kLoop, calls=%fused_computation.7 | loop fusion | flops 524288 | bytes 3145728
  12.8 8.3 %psum.21 = f32[2,2,128]{2,1,0:T(2,128)S(1)} all-reduce(f32[2,2,128]{2,1,0:T(2,128)S(1)} %bitcast.106), channel_id=1, replica_groups=mesh['group'=4,'dp'=2,'tensor'=4] {'tensor'}, use_global_device_ids=true, to_apply=%region_1.0 | all-reduce | flops 512 | bytes 4096 | tf_op jit(solution)/shard_map/psum | solution.py:100
  21.3 2.1 %copy.81 = f32[64,8,8,128]{3,2,1,0:T(8,128)S(1)} copy(f32[64,8,8,128]{3,1,2,0:T(8,128)} %convert_bitcast_fusion) | data formatting | bytes 4194304
  24.1 0.8 fusion.2
  25.1 2.4 %fusion.5 = (bf16[2,2,128,8,128]{4,2,3,1,0:T(8,128)(2,1)S(1)}, f32[2,2,8,128,128]{3,4,2,1,0:T(8,128)}) fusion(f32[2,2,128,8,128]{4,3,2,1,0:T(8,128)S(1)} %bitcast.76, f32[2,2,8,128]{3,2,1,0:T(8,128)S(1)} %get-tuple-element.10, f32[2,2,8,128,192]{3,4,2,1,0:T(8,128)S(1)} %get-tuple-element.11, bf16[2,2,64,8,128]{4,2,3,1,0:T(8,128)(2,1)S(1)} %broadcast_in_dim.56, ...), kind=kOutput, calls=%fused_computation.13 | convolution fusion | flops 207880192 | bytes 9977856 | tf_op jit(solution)/shard_map/cjhqk,cjkhd->cjqhd/dot_general | solution.py:24
  28.3 1.0 broadcast_select_fusion
  29.5 0.9 copy.84
  30.9 1.0 %copy-done.4 = f32[2,8,64,256]{3,2,1,0:T(8,128)} copy-done((f32[2,8,64,256]{3,2,1,0:T(8,128)}, f32[2,8,64,256]{3,2,1,0:T(8,128)S(1)}, u32[]{:S(2)}) %copy-start.4) | copy-done | bytes 1048600
  31.9 1.2 %fusion.39 = (f32[2,8,64]{2,1,0:T(8,128)S(1)}, f32[2,8,64,256]{3,2,1,0:T(8,128)}) fusion(f32[2,8,64,256]{3,2,1,0:T(8,128)S(1)} %fusion.11), kind=kOutput, calls=%fused_computation.77 | output fusion | flops 524543 | bytes 2101248 | tf_op jit(solution)/shard_map/sub | solution.py:63
  33.1 4.5 %multiply_reduce_fusion.1 = (f32[8]{0:T(128)S(1)}, f32[2,64,8]{1,2,0:T(8,128)S(1)}, bf16[2,64,8,128]{3,1,2,0:T(8,128)(2,1)}) fusion(f32[2,64,8,128]{3,2,1,0:T(8,128)} %bitcast.98, f32[8]{0:T(128)S(1)} %copy-done.17, pred[2]{0:T(512)(128)(4,1)S(1)} %copy-done.14, bf16[2,256,8,128]{3,2,1,0:T(8,128)(2,1)S(1)} %bitcast.83, ...), kind=kOutput, calls=%fused_computation.45 | convolution fusion | flops 69075192 | bytes 2891842 | tf_op jit(solution)/shard_map/bhrm,bmhd->brhd/dot_general | solution.py:24
  37.6 2.0 %fusion.12 = bf16[2,8,64,256]{3,2,1,0:T(8,128)(2,1)S(1)} fusion(bf16[2,256,8,128]{3,2,1,0:T(8,128)(2,1)S(1)} %bitcast.84, f32[2,8,64]{2,1,0:T(8,128)S(1)} %bitcast.108, f32[2,8,64,256]{3,2,1,0:T(8,128)} %get-tuple-element.15, f32[2,8,64]{2,1,0:T(8,128)S(1)} %get-tuple-element.14, f32[2,64,8,128]{3,2,1,0:T(8,128)} %bitcast.99, f32[8]{0:T(128)S(1)} %copy-done.17, ...), kind=kOutput, calls=%fused_computation.28 | convolution fusion | flops 68812800 | bytes 3153954 | tf_op jit(solution)/shard_map/brhd,bmhd->bhrm/dot_general | solution.py:24
  40.8 1.9 %fusion.26 = f32[2,8,128,256]{3,2,1,0:T(8,128)} fusion(bf16[2,8,64,256]{3,2,1,0:T(8,128)(2,1)S(1)} %fusion.12, bf16[2,64,8,128]{3,2,1,0:T(8,128)(2,1)S(1)} %bitcast.88), kind=kOutput, calls=%fused_computation.58 | convolution fusion | flops 67108864 | bytes 2883584 | tf_op jit(solution)/shard_map/bhrm,brhd->bmhd/dot_general | solution.py:24
  42.7 6.2 %add_bitcast_fusion.1 = f32[2,256,8,128]{1,3,2,0:T(8,128)} fusion(f32[2,8,128,256]{3,2,1,0:T(8,128)} %fusion.26, f32[2,64,8,128]{3,2,1,0:T(8,128)} %bitcast.100, f32[8]{0:T(128)S(1)} %copy-done.17, pred[2]{0:T(512)(128)(4,1)S(1)} %copy-done.14, f32[2,8,64]{2,1,0:T(8,128)S(1)} %get-tuple-element.14, f32[2,8,64,256]{3,2,1,0:T(8,128)} %copy-done.4), kind=kOutput, calls=%fused_computation.17 | convolution fusion | flops 68814080 | bytes 5771298 | tf_op jit(solution)/shard_map/bhrm,brhd->bmhd/dot_general | solution.py:24
  48.8 2.9 %copy.69 = f32[2,256,8,128]{3,2,1,0:T(8,128)} copy(f32[2,256,8,128]{1,3,2,0:T(8,128)} %add_bitcast_fusion.1) | data formatting | bytes 4194304 | tf_op jit(solution)/shard_map/add | solution.py:78
  51.8 1.9 %convert_element_type.75 = bf16[2,2,128,8,128]{4,3,2,1,0:T(8,128)(2,1)S(1)} convert(f32[2,2,128,8,128]{4,3,2,1,0:T(8,128)} %bitcast.79) | non-fusion elementwise | flops 524288 | bytes 3145728 | tf_op jit(solution)/shard_map/convert_element_type | solution.py:44
  54.0 2.3 %fusion.6 = f32[2,2,128,8]{2,3,1,0:T(8,128)S(1)} fusion(f32[2,2,8,128,128]{3,4,2,1,0:T(8,128)} %get-tuple-element.13, f32[2,2,128,8,128]{4,3,2,1,0:T(8,128)S(1)} %bitcast.81), kind=kLoop, calls=%fused_computation.14 | loop fusion | flops 1044480 | bytes 4210688 | tf_op jit(solution)/shard_map/reduce_sum | solution.py:46
  56.4 1.2 %multiply_convert_fusion = bf16[2,2,8,128,192]{3,4,2,1,0:T(8,128)(2,1)S(1)} fusion(f32[2,2,8,128]{3,2,1,0:T(8,128)S(1)} %bitcast.105, bf16[2,2,64,8,128]{4,2,3,1,0:T(8,128)(2,1)S(1)} %copy-done.6, bf16[2,2,128,8,128]{4,2,3,1,0:T(8,128)(2,1)S(1)} %copy-done.2, bf16[2,2,128,8,128]{4,3,2,1,0:T(8,128)(2,1)S(1)} %convert_element_type.75, ...), kind=kOutput, calls=%fused_computation.2 | convolution fusion | flops 209190912 | bytes 7372800 | tf_op jit(solution)/shard_map/cjqhd,cjkhd->cjhqk/dot_general | solution.py:24
  58.2 0.9 add_bitcast_fusion
  59.1 2.6 %multiply_reduce_fusion = (f32[2,2,128]{2,1,0:T(2,128)S(1)}, f32[2,2,128,8,128]{4,2,3,1,0:T(8,128)}) fusion(f32[2,2,128,8,128]{4,3,2,1,0:T(8,128)S(1)} %bitcast.77, f32[2,2,128]{2,1,0:T(2,128)S(1)} %copy-done.12, f32[8,128]{1,0:T(8,128)S(1)} %bitcast.104, f32[2,2,192,8,128]{4,2,3,1,0:T(8,128)S(1)} %add_bitcast_fusion, ...), kind=kOutput, calls=%fused_computation.16 | convolution fusion | flops 207093248 | bytes 9445376 | tf_op jit(solution)/shard_map/cjhqk,cjkhd->cjqhd/dot_general | solution.py:24
  61.7 22.5 %psum.23 = f32[8]{0:T(128)S(1)} all-reduce(f32[8]{0:T(128)S(1)} %get-tuple-element.5), channel_id=1, replica_groups=mesh['group'=4,'dp'=2,'tensor'=4] {'group','dp'}, use_global_device_ids=true, to_apply=%region_11.12 | all-reduce | flops 8 | bytes 64 | tf_op jit(solution)/shard_map/psum | solution.py:138
  84.2 1.3 %collective-permute-start.3 = (bf16[63,1024]{1,0:T(8,128)(2,1)S(1)}, bf16[63,1024]{1,0:T(8,128)(2,1)S(1)}, u32[]{:S(2)}, u32[]{:S(2)}) collective-permute-start(bf16[63,1024]{1,0:T(8,128)(2,1)S(1)} %slice.42), channel_id=1, source_target_pairs={{0,4},{1,5},{2,6},{3,7},{8,12},{9,13},{10,14},{11,15},{16,20},{17,... | collective-permute-start | bytes 387080 | tf_op jit(solution)/shard_map/ppermute | solution.py:20
  85.5 1.3 %collective-permute-start.1 = (bf16[63,1024]{1,0:T(8,128)(2,1)S(1)}, bf16[63,1024]{1,0:T(8,128)(2,1)S(1)}, u32[]{:S(2)}, u32[]{:S(2)}) collective-permute-start(bf16[63,1024]{1,0:T(8,128)(2,1)S(1)} %slice.40), channel_id=1, source_target_pairs={{0,4},{1,5},{2,6},{3,7},{8,12},{9,13},{10,14},{11,15},{16,20},{17,... | collective-permute-start | bytes 387080 | tf_op jit(solution)/shard_map/ppermute | solution.py:20
  87.7 5.6 %psum.22 = f32[2,2,128]{2,1,0:T(2,128)S(1)} all-reduce(f32[2,2,128]{2,1,0:T(2,128)S(1)} %get-tuple-element.16), channel_id=1, replica_groups=mesh['group'=4,'dp'=2,'tensor'=4] {'tensor'}, use_global_device_ids=true, to_apply=%region_9.10 | all-reduce | flops 512 | bytes 4096 | tf_op jit(solution)/shard_map/psum | solution.py:135
  93.4 3.1 %add_convert_fusion = bf16[2,2,128,8,128]{4,2,3,1,0:T(8,128)(2,1)S(1)} fusion(f32[2,2,128,8,128]{4,2,3,1,0:T(8,128)} %get-tuple-element.17, f32[2,2,128,8,128]{4,3,2,1,0:T(8,128)} %bitcast.80, f32[2,2,128,8,128]{4,3,2,1,0:T(8,128)S(1)} %bitcast.78, f32[2,2,128]{2,1,0:T(2,128)S(1)} %broadcast_multiply_fusion, f32[2,2,128]{2,1,0:T(2,128)S(1)} %copy-done.12), kind=kLoop, calls=%fused_computation.15 | loop fusion | flops 3145728 | bytes 7344128 | tf_op jit(solution)/shard_map/convert_element_type | solution.py:144
  97.2 1.2 %copy.129 = bf16[64,8,8,128]{3,1,2,0:T(8,128)(2,1)} copy(bf16[64,8,8,128]{3,2,1,0:T(8,128)(2,1)S(1)} %bitcast.86) | data formatting | bytes 2097152
  (82 shorter events, 9.5 us)
Async XLA Ops:
  0.6 9.3 %copy-start.3 = (bf16[512,1024]{1,0:T(8,128)(2,1)S(1)}, bf16[512,1024]{1,0:T(8,128)(2,1)}, u32[]{:S(2)}) copy-start(bf16[512,1024]{1,0:T(8,128)(2,1)} %param.9) | copy-start | bytes 3145732
  2.3 26.0 %collective-permute-start.2 = (bf16[63,1024]{1,0:T(8,128)(2,1)}, bf16[63,1024]{1,0:T(8,128)(2,1)}, u32[]{:S(2)}, u32[]{:S(2)}) collective-permute-start(bf16[63,1024]{1,0:T(8,128)(2,1)} %slice.35), channel_id=1, source_target_pairs={{4,0},{5,1},{6,2},{7,3},{12,8},{13,9},{14,10},{15,11},{20,16},{21,... | collective-permute-start | bytes 387080 | tf_op jit(solution)/shard_map/ppermute | solution.py:20
  5.2 23.2 %collective-permute-start = (bf16[63,1024]{1,0:T(8,128)(2,1)}, bf16[63,1024]{1,0:T(8,128)(2,1)}, u32[]{:S(2)}, u32[]{:S(2)}) collective-permute-start(bf16[63,1024]{1,0:T(8,128)(2,1)} %slice.31), channel_id=1, source_target_pairs={{4,0},{5,1},{6,2},{7,3},{12,8},{13,9},{14,10},{15,11},{20,16},{21,... | collective-permute-start | bytes 387080 | tf_op jit(solution)/shard_map/ppermute | solution.py:20
  8.4 3.2 %copy-start.15 = (f32[8]{0:T(128)S(1)}, f32[8]{0:T(128)}, u32[]{:S(2)}) copy-start(f32[8]{0:T(128)} %param.12) | copy-start | bytes 100
  8.4 3.7 %copy-start.13 = (s32[1,4]{1,0:T(1,128)S(1)}, s32[1,4]{1,0:T(1,128)}, u32[]{:S(2)}) copy-start(s32[1,4]{1,0:T(1,128)} %param.10) | copy-start | bytes 52
  8.4 12.8 %copy-start.7 = (bf16[128,1024]{1,0:T(8,128)(2,1)S(1)}, bf16[128,1024]{1,0:T(8,128)(2,1)}, u32[]{:S(2)}) copy-start(bf16[128,1024]{1,0:T(8,128)(2,1)} %param.8) | copy-start | bytes 786436
  21.2 2.2 %copy-start.11 = (f32[2,2,128]{2,1,0:T(2,128)}, f32[2,2,128]{2,1,0:T(2,128)S(1)}, u32[]{:S(2)}) copy-start(f32[2,2,128]{2,1,0:T(2,128)S(1)} %add_rsqrt_fusion) | copy-start | bytes 6148
  21.3 2.1 %copy-start.9 = (f32[1024]{0:T(1024)S(1)}, f32[1024]{0:T(1024)}, u32[]{:S(2)}) copy-start(f32[1024]{0:T(1024)} %param.11) | copy-start | bytes 12292
  23.9 1.0 %copy-start.1 = (bf16[2,2,128,8,128]{4,2,3,1,0:T(8,128)(2,1)}, bf16[2,2,128,8,128]{4,2,3,1,0:T(8,128)(2,1)S(1)}, u32[]{:S(2)}) copy-start(bf16[2,2,128,8,128]{4,2,3,1,0:T(8,128)(2,1)S(1)} %multiply_convert_fusion.1) | copy-start | bytes 3145732
  24.1 1.0 %copy-start.5 = (bf16[2,2,64,8,128]{4,2,3,1,0:T(8,128)(2,1)}, bf16[2,2,64,8,128]{4,2,3,1,0:T(8,128)(2,1)S(1)}, u32[]{:S(2)}) copy-start(bf16[2,2,64,8,128]{4,2,3,1,0:T(8,128)(2,1)S(1)} %broadcast_in_dim.56) | copy-start | bytes 1572868
  24.9 2.6 %copy-start.18 = (f32[2,2,8,128,192]{3,4,2,1,0:T(8,128)}, f32[2,2,8,128,192]{3,4,2,1,0:T(8,128)S(1)}, u32[]{:S(2)}) copy-start(f32[2,2,8,128,192]{3,4,2,1,0:T(8,128)S(1)} %get-tuple-element.11) | copy-start | bytes 9437188
  24.9 2.6 %copy-start.20 = (f32[2,2,8,128]{3,2,1,0:T(8,128)}, f32[2,2,8,128]{3,2,1,0:T(8,128)S(1)}, u32[]{:S(2)}) copy-start(f32[2,2,8,128]{3,2,1,0:T(8,128)S(1)} %get-tuple-element.10) | copy-start | bytes 49156
  30.4 2.7 %copy-start.14 = (pred[2]{0:T(512)(128)(4,1)S(1)}, pred[2]{0:T(512)(128)(4,1)}, u32[]{:S(2)}) copy-start(pred[2]{0:T(512)(128)(4,1)} %get-tuple-element.7) | copy-start | bytes 10
  30.4 2.7 %copy-start.17 = (f32[8]{0:T(128)S(1)}, f32[8]{0:T(128)}, u32[]{:S(2)}) copy-start(f32[8]{0:T(128)} %tanh.3) | copy-start | bytes 100
  30.9 1.0 %copy-start.4 = (f32[2,8,64,256]{3,2,1,0:T(8,128)}, f32[2,8,64,256]{3,2,1,0:T(8,128)S(1)}, u32[]{:S(2)}) copy-start(f32[2,8,64,256]{3,2,1,0:T(8,128)S(1)} %fusion.11) | copy-start | bytes 3145732
  39.5 1.0 copy-start.8
  51.8 2.2 %copy-start = (f32[2,256,8,128]{3,2,1,0:T(8,128)S(1)}, f32[2,256,8,128]{3,2,1,0:T(8,128)}, u32[]{:S(2)}) copy-start(f32[2,256,8,128]{3,2,1,0:T(8,128)} %copy.69) | copy-start | bytes 6291460
  51.8 4.6 %copy-start.19 = (f32[2,2,8,128,192]{3,4,2,1,0:T(8,128)S(1)}, f32[2,2,8,128,192]{3,4,2,1,0:T(8,128)}, u32[]{:S(2)}) copy-start(f32[2,2,8,128,192]{3,4,2,1,0:T(8,128)} %copy-done.18) | copy-start | bytes 9437188
  54.0 2.3 %copy-start.2 = (bf16[2,2,128,8,128]{4,2,3,1,0:T(8,128)(2,1)S(1)}, bf16[2,2,128,8,128]{4,2,3,1,0:T(8,128)(2,1)}, u32[]{:S(2)}) copy-start(bf16[2,2,128,8,128]{4,2,3,1,0:T(8,128)(2,1)} %copy-done.1) | copy-start | bytes 3145732
  54.0 2.4 %copy-start.6 = (bf16[2,2,64,8,128]{4,2,3,1,0:T(8,128)(2,1)S(1)}, bf16[2,2,64,8,128]{4,2,3,1,0:T(8,128)(2,1)}, u32[]{:S(2)}) copy-start(bf16[2,2,64,8,128]{4,2,3,1,0:T(8,128)(2,1)} %copy-done.5) | copy-start | bytes 1572868
  54.0 2.4 %copy-start.21 = (f32[2,2,8,128]{3,2,1,0:T(8,128)S(1)}, f32[2,2,8,128]{3,2,1,0:T(8,128)}, u32[]{:S(2)}) copy-start(f32[2,2,8,128]{3,2,1,0:T(8,128)} %copy-done.20) | copy-start | bytes 49156
  58.1 0.9 copy-start.10
  58.1 0.9 copy-start.12
  84.2 14.8 %collective-permute-start.3 = (bf16[63,1024]{1,0:T(8,128)(2,1)S(1)}, bf16[63,1024]{1,0:T(8,128)(2,1)S(1)}, u32[]{:S(2)}, u32[]{:S(2)}) collective-permute-start(bf16[63,1024]{1,0:T(8,128)(2,1)S(1)} %slice.42), channel_id=1, source_target_pairs={{0,4},{1,5},{2,6},{3,7},{8,12},{9,13},{10,14},{11,15},{16,20},{17,... | collective-permute-start | bytes 387080 | tf_op jit(solution)/shard_map/ppermute | solution.py:20
  85.5 14.3 %collective-permute-start.1 = (bf16[63,1024]{1,0:T(8,128)(2,1)S(1)}, bf16[63,1024]{1,0:T(8,128)(2,1)S(1)}, u32[]{:S(2)}, u32[]{:S(2)}) collective-permute-start(bf16[63,1024]{1,0:T(8,128)(2,1)S(1)} %slice.40), channel_id=1, source_target_pairs={{0,4},{1,5},{2,6},{3,7},{8,12},{9,13},{10,14},{11,15},{16,20},{17,... | collective-permute-start | bytes 387080 | tf_op jit(solution)/shard_map/ppermute | solution.py:20
  96.5 2.0 %copy-start.16 = (f32[8]{0:T(128)S(1)}, f32[8]{0:T(128)}, u32[]{:S(2)}) copy-start(f32[8]{0:T(128)} %param.12) | copy-start | bytes 100
where the time goes:
time: 101 us
  blocking collectives  36.5 us (36%)
  matrix products  23.7 us (23%)
  local copies, waits for them, and re-layouts  17.9 us (18%)
  other arithmetic  16.2 us (16%)
  starting transfers between devices  5.14 us (5%)
  between operations  1.11 us (1%)
    dot_general x12, matrix products, product(): return jnp.einsum(form, left, right, preferred_element_type=jnp.float32)  23.7 us
    psum x1, blocking collectives, shards(): summed = lax.psum(gate_terms, ('group', 'dp'))  22.5 us
    psum x1, blocking collectives, shards(): square_sum = lax.psum(jnp.sum(floats * floats, axis=(3, 4)), 'tensor')  8.34 us
    unnamed x54, local copies, waits for them, and re-layouts  7.17 us
    psum x1, blocking collectives, shards(): lax.psum(jnp.sum(gain_grad * scaled, axis=(3, 4)), 'tensor') / full_width  5.63 us
    ppermute x4, starting transfers between devices, shifted(): lax.ppermute(value, axis, [(source, source + steps) for source in range(l...  5.14 us
    slice x2, local copies, waits for them, and re-layouts, shards(): incoming = shifted((queries[:lead], out_grad[:lead]), 'dp', -1)  3.23 us
    convert_element_type x1, other arithmetic, shards(): neighbour_grad.reshape(-1, local_width).astype(jnp.bfloat16)  3.13 us
  transfers between devices with their start and end apart: 4, of which 0 were waited for; matrix products, arithmetic and copies ran while one was open for 22% of the time, Pallas kernels for 0%

commit v1 on v0

v1 whole, which is shorter than its diff:
```python
import functools
import math

import jax
import jax.numpy as jnp
from jax import lax
from jax.experimental import pallas as pl
from jax.experimental.pallas import tpu as pltpu
from jax.sharding import PartitionSpec as P

CH = 64
NB = 2
NL = 128
UNROLL = 2

epsilon = 1e-05
masked_score = -1e30
MESH = pl.DeviceIdType.MESH
F32 = jnp.float32
BF16 = jnp.bfloat16


def nn(left, right):
    return lax.dot_general(left, right, (((1,), (0,)), ((), ())), preferred_element_type=F32)


def nt(left, right):
    return lax.dot_general(left, right, (((1,), (1,)), ((), ())), preferred_element_type=F32)


def tn(left, right):
    return lax.dot_general(left, right, (((0,), (0,)), ((), ())), preferred_element_type=F32)


def kernel(
    sizes,
    q_in, c_in, x_in, counts, gains, gates, og_in,
    out_o, qg_o, sg_o, ng_o, gate_o,
    x_v, c_v, q_v, og_v, halo, qf, ogf, sb, ss, ss_got, inv, pacc, pj, pj_got,
    a_v, ng_v, sg_v, outf, qgf, ret, arr, outb, qgb, gate_buf,
    in_sem, out_sem, halo_s, halo_r, ss_s, ss_r, pj_s, pj_r, ret_s, ret_r, gate_s, gate_r,
):
    n_group, n_dp, n_tensor, heads, hd, rows, seq_spans = sizes
    spans = rows // CH
    lead = CH - 1
    width = heads * hd
    full_width = n_tensor * width
    blocks = spans * NB
    span_rows = NB * NL
    group = lax.axis_index("group")
    dp = lax.axis_index("dp")
    tensor = lax.axis_index("tensor")
    lines = n_group * n_dp
    line = group * n_dp + dp
    first_span = dp * spans
    order = [spans - 1] + list(range(spans - 1))

    def line_peer(d):
        flat = lax.rem(line + d, lines)
        return {"group": flat // n_dp, "dp": lax.rem(flat, n_dp), "tensor": tensor}

    def tensor_peer(d):
        return {"group": group, "dp": dp, "tensor": lax.rem(tensor + d, n_tensor)}

    before = {"group": group, "dp": lax.rem(dp + n_dp - 1, n_dp), "tensor": tensor}
    after = {"group": group, "dp": lax.rem(dp + 1, n_dp), "tensor": tensor}

    def remote(src, dst, send, recv, device):
        return pltpu.make_async_remote_copy(
            src_ref=src, dst_ref=dst, send_sem=send, recv_sem=recv,
            device_id=device, device_id_type=MESH,
        )

    loads = []
    for at, c in enumerate(order):
        piece = pl.ds(c * span_rows, span_rows)
        loads.append(pltpu.make_async_copy(x_in.at[piece], x_v.at[piece], in_sem.at[at]))
    small = [
        pltpu.make_async_copy(q_in, q_v, in_sem.at[spans]),
        pltpu.make_async_copy(og_in, og_v, in_sem.at[spans + 1]),
        pltpu.make_async_copy(c_in, c_v, in_sem.at[spans + 2]),
    ]
    for copy in loads + small:
        copy.start()

    barrier = pltpu.get_barrier_semaphore()
    for d in range(1, n_tensor):
        pl.semaphore_signal(barrier, inc=1, device_id=tensor_peer(d), device_id_type=MESH)
    for d in range(1, lines):
        pl.semaphore_signal(barrier, inc=1, device_id=line_peer(d), device_id_type=MESH)

    def row_sums(value):
        return jnp.sum(value.T, axis=0, keepdims=True)

    def row_spread(line_value):
        return jnp.broadcast_to(line_value, (NL, NL)).T

    for at, c in enumerate(order):
        loads[at].wait()
        for j in range(NB):
            b = c * NB + j
            piece = pl.ds(b * NL, NL)
            total = jnp.zeros((NL, hd), F32)
            for h in range(heads):
                part = x_v[piece, h * hd:(h + 1) * hd].astype(F32)
                total = total + part * part
            ss[b:b + 1, :] = row_sums(total)

    pl.semaphore_wait(barrier, n_tensor - 1 + lines - 1)

    halo_copies = [
        remote(q_in.at[pl.ds(0, CH)], halo.at[0], halo_s.at[0], halo_r.at[0], before),
        remote(og_in.at[pl.ds(0, CH)], halo.at[1], halo_s.at[1], halo_r.at[1], before),
    ]
    ss_copies = [
        remote(ss, ss_got.at[d - 1], ss_s.at[d - 1], ss_r.at[d - 1], tensor_peer(d))
        for d in range(1, n_tensor)
    ]
    for copy in ss_copies + halo_copies:
        copy.start()

    small[0].wait()
    small[1].wait()
    small[2].wait()
    qf[0:rows, :] = q_v[...].astype(F32)
    ogf[0:rows, :] = og_v[...].astype(F32)
    pacc[...] = jnp.zeros_like(pacc)
    gate_buf[line] = jnp.zeros((heads, hd), F32)

    for copy in ss_copies:
        copy.wait()
    square = ss[...]
    for d in range(1, n_tensor):
        square = square + ss_got[d - 1]
    inv[...] = lax.rsqrt(square / full_width + epsilon)
    for b in range(blocks):
        sb[b * NL:(b + 1) * NL, :] = row_spread(inv[b:b + 1, :])

    for copy in halo_copies:
        copy.wait()
    follows = lax.rem(first_span + spans, seq_spans) != 0
    qf[rows:rows + CH, :] = jnp.where(follows, halo[0].astype(F32), 0.0)
    ogf[rows:rows + CH, :] = jnp.where(follows, halo[1].astype(F32), 0.0)

    enc_scale = math.log2(math.e) / hd
    scale = 1.0 / math.sqrt(hd)

    def unit(c, h, usable, present):
        cols = pl.ds(pl.multiple_of(h * hd, hd), hd)
        g = gains[pl.ds(h, 1), :]
        gt = jnp.tanh(jnp.full((1, hd), gates[h], F32))
        context = c_v[c * CH:(c + 1) * CH, cols]
        slots = []
        for j in range(NB):
            base = c * span_rows + j * NL
            x = x_v[base:base + NL, cols].astype(F32)
            normed = (x * sb[base:base + NL, :] * g).astype(BF16)
            keys = jnp.concatenate([normed, context], axis=0)
            powers = jnp.exp2(nt(keys, normed) * enc_scale)
            weights = powers * (1.0 / jnp.sum(powers, axis=0, keepdims=True))
            rounded = weights.astype(BF16)
            encoded = (x + tn(rounded, keys)).astype(BF16)
            slots.append((base, normed, keys, weights, rounded, encoded))
        enc = jnp.concatenate([slot[5] for slot in slots], axis=0)
        at = lead + c * CH
        og = ogf[at:at + CH, cols]
        query = qf[at:at + CH, cols].astype(BF16)
        pair = jnp.concatenate([(gt * og).astype(BF16), query], axis=0)
        both = nt(pair, enc)
        grad_weights = both[:CH]
        scores = jnp.where(usable, both[CH:] * scale, masked_score)
        powers = jnp.exp(scores - jnp.max(scores, axis=1, keepdims=True))
        weights = powers * (present / jnp.sum(powers, axis=1, keepdims=True))
        rounded = weights.astype(BF16)
        offset = jnp.sum(rounded.astype(F32) * grad_weights, axis=1, keepdims=True)
        score_grad = (weights * (grad_weights - offset) * scale).astype(BF16)
        coefficients = jnp.concatenate([rounded, score_grad], axis=0)
        mixed = nn(coefficients, enc)
        attended = mixed[:CH]
        out = gt * attended
        outf[CH + c * CH:2 * CH + c * CH, cols] = out
        qgf[CH + c * CH:2 * CH + c * CH, cols] = mixed[CH:]
        if c == spans - 1:
            ret[0, :, cols] = out.astype(BF16)
            ret[1, :, cols] = mixed[CH:].astype(BF16)
        gate_buf[line, pl.ds(h, 1), :] += jnp.sum(og * attended, axis=0, keepdims=True)
        enc_grad = tn(coefficients, pair)
        span_grad = jnp.zeros((CH, hd), F32)
        for j in range(NB):
            base, normed, keys, weights, rounded, _ = slots[j]
            grad = enc_grad[j * NL:(j + 1) * NL]
            grad_rounded = grad.astype(BF16)
            grad_weights = nt(keys, grad_rounded)
            offset = jnp.sum(rounded.astype(F32) * grad_weights, axis=0, keepdims=True)
            score_grad = (weights * (grad_weights - offset) * (1.0 / hd)).astype(BF16)
            key_grad = nn(
                jnp.concatenate([score_grad, rounded], axis=1),
                jnp.concatenate([normed, grad_rounded], axis=0),
            )
            gained = (tn(score_grad, keys) + key_grad[:NL]) * g
            span_grad = span_grad + key_grad[NL:]
            x = x_v[base:base + NL, cols].astype(F32)
            pacc[base:base + NL, :] += gained * x
            a_v[base:base + NL, cols] = grad + sb[base:base + NL, :] * gained
        sg_v[c * CH:(c + 1) * CH, cols] = span_grad.astype(BF16)

    def project(slot):
        return [
            remote(pj.at[slot], pj_got.at[slot, d - 1], pj_s.at[slot, d - 1],
                   pj_r.at[slot, d - 1], tensor_peer(d))
            for d in range(1, n_tensor)
        ]

    def finish(slot, c):
        total = pj[slot]
        for d in range(1, n_tensor):
            total = total + pj_got[slot, d - 1]
        s = inv[c * NB:(c + 1) * NB, :]
        factor = s * s * s * total / full_width
        for j in range(NB):
            base = c * span_rows + j * NL
            spread = row_spread(factor[j:j + 1, :])
            for h in range(heads):
                cols = slice(h * hd, (h + 1) * hd)
                x = x_v[base:base + NL, cols].astype(F32)
                ng_v[base:base + NL, cols] = (a_v[base:base + NL, cols] - x * spread).astype(BF16)
        piece = pl.ds(c * span_rows, span_rows)
        copy = pltpu.make_async_copy(ng_v.at[piece], ng_o.at[piece], out_sem.at[slot])
        copy.start()
        return copy

    ret_copies = [
        remote(ret.at[i], arr.at[i], ret_s.at[i], ret_r.at[i], after) for i in range(2)
    ]
    pj_copies = []
    for slot, c in enumerate(order):
        index = first_span + c
        count = counts[index // seq_spans, lax.rem(index, seq_spans)]
        usable = lax.broadcasted_iota(jnp.int32, (CH, span_rows), 1) // NL < count
        present = jnp.where(count > 0, 1.0, 0.0).astype(F32)

        def step(i, carry):
            for u in range(UNROLL):
                unit(c, i * UNROLL + u, usable, present)
            return carry

        lax.fori_loop(0, heads // UNROLL, step, 0)
        for j in range(NB):
            base = c * span_rows + j * NL
            pj[slot, j:j + 1, :] = row_sums(pacc[base:base + NL, :])
        copies = project(slot)
        for copy in copies:
            copy.start()
        pj_copies.append(copies)
        if slot == 0:
            for copy in ret_copies:
                copy.start()

    gate_copies = [
        remote(gate_buf.at[line], gate_buf.at[line], gate_s.at[d - 1], gate_r.at[d - 1], line_peer(d))
        for d in range(1, lines)
    ]
    for copy in gate_copies:
        copy.start()
    done = [pltpu.make_async_copy(sg_v, sg_o, out_sem.at[spans])]
    done[0].start()
    for slot in range(spans - 1):
        for copy in pj_copies[slot]:
            copy.wait()
        done.append(finish(slot, order[slot]))
    for copy in ret_copies:
        copy.wait()
    starts = lax.rem(first_span, seq_spans) == 0
    outf[0:CH, :] = jnp.where(starts, 0.0, arr[0].astype(F32))
    qgf[0:CH, :] = jnp.where(starts, 0.0, arr[1].astype(F32))
    outb[...] = outf[1:rows + 1, :].astype(BF16)
    qgb[...] = qgf[1:rows + 1, :].astype(BF16)
    for i, (source, target) in enumerate([(outb, out_o), (qgb, qg_o)]):
        copy = pltpu.make_async_copy(source, target, out_sem.at[spans + 1 + i])
        copy.start()
        done.append(copy)
    for copy in pj_copies[spans - 1]:
        copy.wait()
    done.append(finish(spans - 1, order[spans - 1]))
    for copy in gate_copies:
        copy.wait()
    summed = gate_buf[0]
    for i in range(1, lines):
        summed = summed + gate_buf[i]
    tokens = n_group * n_dp * rows
    for h in range(heads):
        t = jnp.tanh(jnp.full((1, hd), gates[h], F32))
        gate_o[h] = jnp.sum((1.0 - t * t) * summed[h:h + 1, :]) * (1.0 / math.sqrt(tokens))
    for copy in done:
        copy.wait()


def shards(queries, span_state, neigh_state, counts, norm_gain, head_gate, out_grad):
    heads = head_gate.shape[0]
    rows, width = queries.shape
    hd = width // heads
    n_group, n_dp, n_tensor = (lax.axis_size(a) for a in ("group", "dp", "tensor"))
    spans = rows // CH
    blocks = spans * NB
    tokens = neigh_state.shape[0]
    lines = n_group * n_dp
    sizes = (n_group, n_dp, n_tensor, heads, hd, rows, counts.shape[1])
    others = max(1, n_tensor - 1)
    any_space = pl.BlockSpec(memory_space=pl.ANY)
    smem = pl.BlockSpec(memory_space=pltpu.SMEM)
    vmem = pl.BlockSpec(memory_space=pltpu.VMEM)
    dma = pltpu.SemaphoreType.DMA
    return pl.pallas_call(
        functools.partial(kernel, sizes),
        out_shape=(
            jax.ShapeDtypeStruct((rows, width), BF16),
            jax.ShapeDtypeStruct((rows, width), BF16),
            jax.ShapeDtypeStruct((rows, width), BF16),
            jax.ShapeDtypeStruct((tokens, width), BF16),
            jax.ShapeDtypeStruct((heads,), F32),
        ),
        in_specs=[any_space, any_space, any_space, smem, vmem, smem, any_space],
        out_specs=(any_space, any_space, any_space, any_space, smem),
        scratch_shapes=[
            pltpu.VMEM((tokens, width), BF16),
            pltpu.VMEM((rows, width), BF16),
            pltpu.VMEM((rows, width), BF16),
            pltpu.VMEM((rows, width), BF16),
            pltpu.VMEM((2, CH, width), BF16),
            pltpu.VMEM((rows + CH, width), F32),
            pltpu.VMEM((rows + CH, width), F32),
            pltpu.VMEM((tokens, hd), F32),
            pltpu.VMEM((blocks, NL), F32),
            pltpu.VMEM((others, blocks, NL), F32),
            pltpu.VMEM((blocks, NL), F32),
            pltpu.VMEM((tokens, hd), F32),
            pltpu.VMEM((spans, NB, NL), F32),
            pltpu.VMEM((spans, others, NB, NL), F32),
            pltpu.VMEM((tokens, width), F32),
            pltpu.VMEM((tokens, width), BF16),
            pltpu.VMEM((rows, width), BF16),
            pltpu.VMEM((rows + CH, width), F32),
            pltpu.VMEM((rows + CH, width), F32),
            pltpu.VMEM((2, CH, width), BF16),
            pltpu.VMEM((2, CH, width), BF16),
            pltpu.VMEM((rows, width), BF16),
            pltpu.VMEM((rows, width), BF16),
            pltpu.VMEM((lines, heads, hd), F32),
            dma((spans + 3,)),
            dma((spans + 3,)),
            dma((2,)),
            dma((2,)),
            dma((others,)),
            dma((others,)),
            dma((spans, others)),
            dma((spans, others)),
            dma((2,)),
            dma((2,)),
            dma((max(1, lines - 1),)),
            dma((max(1, lines - 1),)),
        ],
        compiler_params=pltpu.CompilerParams(collective_id=0, has_side_effects=True),
    )(queries, span_state, neigh_state, counts, norm_gain.reshape(heads, hd), head_gate, out_grad)


def solution(mesh):
    rows = P(("group", "dp"), "tensor")
    return jax.shard_map(
        shards,
        mesh=mesh,
        in_specs=(rows, rows, rows, P("group", None), P("tensor"), P("tensor"), rows),
        out_specs=(rows, rows, rows, rows, P("tensor")),
        check_vma=False,
    )
```

time: 101 us -> 53.1 us (0.53)
  Pallas kernels: 0 us -> 45.7 us
  blocking collectives: 36.5 us -> 0 us
  matrix products: 23.7 us -> 0 us
  other arithmetic: 16.2 us -> 0 us
  local copies, waits for them, and re-layouts: 17.9 us -> 6.58 us
  starting transfers between devices: 5.14 us -> 0 us
    pallas_call x0 -> x1, Pallas kernels: none -> 45.7 us  [shards(): pl.pallas_call(functools.partial(kernel, sizes), out_shape=(jax.ShapeDtyp...]
    psum x3 -> x0, blocking collectives: 36.5 us -> none  [the longest x1 22.5 us: shards(): summed = lax.psum(gate_terms, ('group', 'dp'))]
    dot_general x12 -> x0, matrix products: 23.7 us -> none  [product(): return jnp.einsum(form, left, right, preferred_element_type=jnp.float32)]
    convert_element_type x3 -> x0, other arithmetic: 5.55 us -> none  [the longest x1 3.13 us: shards(): neighbour_grad.reshape(-1, local_width).astype(jnp.bfloat16)]
    slice x8 -> x0, local copies, waits for them, and re-layouts: 5.22 us -> none  [the longest x2 3.23 us: shards(): incoming = shifted((queries[:lead], out_grad[:lead]), 'dp', -1)]
    ppermute x4 -> x0, starting transfers between devices: 5.14 us -> none  [shifted(): lax.ppermute(value, axis, [(source, source + steps) for source in range(l...]
    reduce_sum x3 -> x0, other arithmetic: 3.93 us -> none  [the longest x1 2.32 us: encoder_backward(): jnp.sum(grad_encoded * mixture, axis=-1)]
    add x1 -> x0, local copies, waits for them, and re-layouts: 2.93 us -> none  [cross_attend(): product('bhrm,brhd->bmhd', score_grad, blocks)]
  transfers between devices with their start and end apart: 4 -> 0, of which waited for: 0 -> 0; matrix products, arithmetic and copies ran while one was open for 22% -> 0% of each run, Pallas kernels for 0% -> 0%
where the time goes in v1:
time: 53.1 us; the launch traced here: 52.9 us
  Pallas kernels  45.7 us (86%)
  local copies, waits for them, and re-layouts  6.58 us (12%)
  between operations  0.65 us (1%)
    pallas_call x1, Pallas kernels, shards(): pl.pallas_call(functools.partial(kernel, sizes), out_shape=(jax.ShapeDtyp...  45.7 us
    unnamed x9, local copies, waits for them, and re-layouts  6.58 us

profile of v1, /device:TPU:0, one launch (start us, length us, event | category | flops | bytes accessed | tf_op | source)
XLA Modules:
  0.0 52.9 jit_solution(4096823489191277722)
XLA Ops:
  0.6 45.7 %shard_map.110 = (bf16[128,1024]{1,0:T(8,128)(2,1)}, bf16[128,1024]{1,0:T(8,128)(2,1)}, bf16[128,1024]{1,0:T(8,128)(2,1)}, bf16[512,1024]{1,0:T(8,128)(2,1)}, f32[8]{0:T(128)}) custom-call(bf16[128,1024]{1,0:T(8,128)(2,1)} %q_in.1, bf16[128,1024]{1,0:T(8,128)(2,1)} %c_in.1, bf16[512,1024]{1,0:T(8,128)(2,1)} %x_in.1, s32[1,4]{1,0:T(1,128)} %counts.1, ...), custom_call_target="tpu_custom_call" | custom-call | tf_op jit(solution)/shard_map/pallas_call | solution.py:313
  46.3 0.0 copy-start
  46.3 1.8 %copy.17 = bf16[128,1024]{1,0:T(8,128)(2,1)} copy(bf16[128,1024]{1,0:T(8,128)(2,1)} %get-tuple-element.10) | data formatting | bytes 524288
  48.1 1.7 %copy.18 = bf16[128,1024]{1,0:T(8,128)(2,1)} copy(bf16[128,1024]{1,0:T(8,128)(2,1)} %get-tuple-element.11) | data formatting | bytes 524288
  49.7 1.7 %copy.19 = bf16[128,1024]{1,0:T(8,128)(2,1)} copy(bf16[128,1024]{1,0:T(8,128)(2,1)} %get-tuple-element.12) | data formatting | bytes 524288
  51.4 0.0 copy-done
  51.4 0.0 copy-start.1
  51.4 1.0 %copy.20 = bf16[512,1024]{1,0:T(8,128)(2,1)} copy(bf16[512,1024]{1,0:T(8,128)(2,1)S(1)} %copy-done) | data formatting | bytes 2097152
  52.4 0.0 copy-done.1
  52.4 0.5 copy.21
Async XLA Ops:
  46.3 5.1 %copy-start = (bf16[512,1024]{1,0:T(8,128)(2,1)S(1)}, bf16[512,1024]{1,0:T(8,128)(2,1)}, u32[]{:S(2)}) copy-start(bf16[512,1024]{1,0:T(8,128)(2,1)} %get-tuple-element.13) | copy-start | bytes 3145732
  51.4 1.0 %copy-start.1 = (f32[8]{0:T(128)S(1)}, f32[8]{0:T(128)}, u32[]{:S(2)}) copy-start(f32[8]{0:T(128)} %get-tuple-element.14) | copy-start | bytes 100
